TPU v7x, 32 devices: a whole 2x2x4 slice. The times are simulated.
32 devices in a mesh: tm: 2 (over x), grid: 16 (over z, y, core).
Axes of the slice: x: 2, y: 2, z: 4, core: 2. Of those that a mesh axis runs over, the one named last changes fastest.
Arguments:
- occupied_green: bfloat16 [2, 1024, 1024], P('tm', 'grid'), may hold values from -0.005859375 to 0.005859375
- empty_green: bfloat16 [2, 1024, 1024], P('tm', 'grid'), may hold values from -0.005859375 to 0.005859375
- basis: bfloat16 [12288, 1024], P('grid'), may hold values from -8 to 8
- time_weights: float32 [2, 2], replicated, may hold values from 0.25 to 1
Outputs:
- polarizability: float32 [2, 1024, 1024], P('tm', 'grid')
All inputs are finite; a program needn't handle non-finite values.
Results may differ from a plain program's by a relative error of at most 0.0012.
Values may be sent and summed in bfloat16 or wider, within the bound.
A program may use at most 128 MiB of HBM per device.

v0:
```python
import jax
import jax.numpy as jnp
from jax import lax
from jax.sharding import PartitionSpec as P

NR = 12288
NB = 1024


def weigh_times(time_weights, block_list, scale_factor):
    time_count = len(block_list)
    group_index = lax.axis_index("tm")
    weights_local = lax.dynamic_slice_in_dim(time_weights, group_index * time_count, time_count, 1)
    accum = weights_local[:, 0, None, None] * block_list[0][None]
    return scale_factor * accum


def step_size(piece_rows):
    return max((divisor for divisor in range(1, 2049) if piece_rows % divisor == 0))


def shards(occupied_green, empty_green, basis, time_weights):
    stacked = jnp.stack([occupied_green, empty_green])
    time_count = occupied_green.shape[0]
    coef_block = occupied_green.shape[1]
    row_total = basis.shape[0]
    scale_factor = 1.0 / NR

    def make_accumulate(combined_rows):

        def accumulate(running, basis_piece, first_row):
            piece_rows = basis_piece.shape[0]
            step_rows = step_size(piece_rows)

            def one_step(step_index, inner):
                basis_subpart = lax.dynamic_slice_in_dim(
                    basis_piece, step_index * step_rows, step_rows, 0
                )
                real_pair = jnp.einsum(
                    "qoa,ba->qob", combined_rows, basis_subpart, preferred_element_type=jnp.float32
                )
                product = (real_pair[0] * real_pair[1]).astype(jnp.bfloat16)
                return inner + jnp.dot(product, basis_subpart, preferred_element_type=jnp.float32)

            return lax.fori_loop(0, piece_rows // step_rows, one_step, running)

        return accumulate

    initial = jnp.zeros((time_count * row_total, NB), jnp.float32)
    projected = jnp.einsum(
        "sl,ftkl->ftsk",
        basis,
        lax.all_gather(stacked, "grid", axis=2, tiled=True),
        preferred_element_type=jnp.float32,
    ).astype(jnp.bfloat16)
    combined_rows = projected.reshape(2, time_count * row_total, NB)
    accumulate = make_accumulate(combined_rows)
    summed = accumulate(initial, lax.all_gather(basis, "grid", axis=0, tiled=True), jnp.int32(0))
    back_half = summed.astype(jnp.bfloat16).reshape(time_count, row_total, NB)
    coef_rows = lax.psum_scatter(
        jnp.einsum("tsk,sl->ktl", back_half, basis, preferred_element_type=jnp.float32).reshape(
            lax.axis_size("grid") * coef_block, time_count * NB
        ),
        "grid",
        scatter_dimension=0,
        tiled=True,
    ).reshape(coef_block, time_count, NB)
    block_list = [coef_rows[:, 0]]
    result = lax.psum_scatter(
        weigh_times(time_weights, block_list, scale_factor), "tm", scatter_dimension=0, tiled=True
    )
    return result


def solution(mesh):
    in_specs = (P("tm", "grid", None), P("tm", "grid", None), P("grid", None), P())
    out_specs = P("tm", "grid", None)
    return jax.shard_map(shards, mesh=mesh, in_specs=in_specs, out_specs=out_specs, check_vma=False)
```

profile of v0, /device:TPU:0, one launch (start us, length us, event | category | flops | bytes accessed | tf_op | source)
XLA Modules:
  0.0 431.6 jit_solution(16188916720244867342)
XLA Ops:
  6.5 1.7 pad_maximum_fusion
  8.3 0.7 all-gather.3.cloned.1.call-update
  9.1 53.6 %all-gather.5.cloned.1.call-done = bf16[2,1,1024,1024]{3,2,0,1:T(8,128)(2,1)} async-done(((bf16[2,1,64,1024]{3,2,0,1:T(8,128)(2,1)}), bf16[2,1,1024,1024]{3,2,0,1:T(8,128)(2,1)}) %all-gather.5.cloned.1.call-update) | async-done | bytes 4194320 | tf_op jit(solution)/shard_map/all_gather | solution.py:53
  62.7 7.9 %convert_bitcast_fusion = bf16[2,768,1024]{1,2,0:T(8,128)(2,1)} fusion(bf16[2,1,1024,1024]{3,2,0,1:T(8,128)(2,1)} %all-gather.5.cloned.1.call-done, bf16[768,1024]{1,0:T(8,128)(2,1)} %param.8), kind=kOutput, calls=%fused_computation.13 | convolution fusion | flops 3222798336 | bytes 8912896 | tf_op jit(solution)/shard_map/sl,ftkl->ftsk/dot_general | solution.py:50
  70.5 3.2 copy.5
  73.8 117.6 %all-gather.3.cloned.1.call-done = bf16[12288,1024]{1,0:T(8,128)(2,1)} async-done(((bf16[768,1024]{1,0:T(8,128)(2,1)}), bf16[12288,1024]{1,0:T(8,128)(2,1)}) %all-gather.3.cloned.1.call-update) | async-done | bytes 25165840 | tf_op jit(solution)/shard_map/all_gather | solution.py:58
  191.3 138.8 %while.14 = (s32[]{:T(128)}, f32[768,1024]{1,0:T(8,128)}, bf16[12288,1024]{1,0:T(8,128)(2,1)}, bf16[2,768,1024]{2,1,0:T(8,128)(2,1)S(1)}, s32[]{:T(128)}, /*index=5*/s32[]{:T(128)}, s32[]{:T(128)}, s32[]{:T(128)}) while((s32[]{:T(128)}, f32[768,1024]{1,0:T(8,128)}, bf16[12288,1024]{1,0:T(8,128)(2,1)}, ...), condition=%wide.region_1.0_spmd.clone, body=%wide.region_0.0_spmd.clone.sunk | while | flops 9668395008 | bytes 42991772 | solution.py:45
  191.4 11.5 %convolution_bitcast_fusion.2 = f32[2,768,2048]{1,2,0:T(8,128)} fusion(bf16[2,768,1024]{2,1,0:T(8,128)(2,1)S(1)} %get-tuple-element.156, bf16[12288,1024]{1,0:T(8,128)(2,1)} %get-tuple-element.155, s32[]{:T(128)S(6)} %select_n.13), kind=kOutput, calls=%fused_computation.2.clone.1 | convolution fusion | flops 6442450944 | bytes 19922948 | tf_op jit(solution)/shard_map/while/body/eval_jaxpr/qoa,ba->qob/dot_general | solution.py:39
  202.9 10.9 %select_add_fusion.2 = f32[768,1024]{1,0:T(8,128)} fusion(f32[768,1024]{1,0:T(8,128)} %get-tuple-element.146, bf16[12288,1024]{1,0:T(8,128)(2,1)} %get-tuple-element.155, s32[]{:T(128)S(6)} %select_n.13, f32[2,768,2048]{1,2,0:T(8,128)} %convolution_bitcast_fusion.2, pred[]{:T(512)S(6)} %compare.3), kind=kOutput, calls=%fused_computation.8.clone.1 | convolution fusion | flops 3225944064 | bytes 23068676 | tf_op jit(solution)/shard_map/while/body/eval_jaxpr/dot_general | solution.py:43
  213.7 11.5 %convolution_bitcast_fusion.2 = f32[2,768,2048]{1,2,0:T(8,128)} fusion(bf16[2,768,1024]{2,1,0:T(8,128)(2,1)S(1)} %get-tuple-element.156, bf16[12288,1024]{1,0:T(8,128)(2,1)} %get-tuple-element.155, s32[]{:T(128)S(6)} %select_n.13), kind=kOutput, calls=%fused_computation.2.clone.1 | convolution fusion | flops 6442450944 | bytes 19922948 | tf_op jit(solution)/shard_map/while/body/eval_jaxpr/qoa,ba->qob/dot_general | solution.py:39
  225.2 11.8 %select_add_fusion.2 = f32[768,1024]{1,0:T(8,128)} fusion(f32[768,1024]{1,0:T(8,128)} %get-tuple-element.146, bf16[12288,1024]{1,0:T(8,128)(2,1)} %get-tuple-element.155, s32[]{:T(128)S(6)} %select_n.13, f32[2,768,2048]{1,2,0:T(8,128)} %convolution_bitcast_fusion.2, pred[]{:T(512)S(6)} %compare.3), kind=kOutput, calls=%fused_computation.8.clone.1 | convolution fusion | flops 3225944064 | bytes 23068676 | tf_op jit(solution)/shard_map/while/body/eval_jaxpr/dot_general | solution.py:43
  237.0 11.5 %convolution_bitcast_fusion.2 = f32[2,768,2048]{1,2,0:T(8,128)} fusion(bf16[2,768,1024]{2,1,0:T(8,128)(2,1)S(1)} %get-tuple-element.156, bf16[12288,1024]{1,0:T(8,128)(2,1)} %get-tuple-element.155, s32[]{:T(128)S(6)} %select_n.13), kind=kOutput, calls=%fused_computation.2.clone.1 | convolution fusion | flops 6442450944 | bytes 19922948 | tf_op jit(solution)/shard_map/while/body/eval_jaxpr/qoa,ba->qob/dot_general | solution.py:39
  248.5 11.8 %select_add_fusion.2 = f32[768,1024]{1,0:T(8,128)} fusion(f32[768,1024]{1,0:T(8,128)} %get-tuple-element.146, bf16[12288,1024]{1,0:T(8,128)(2,1)} %get-tuple-element.155, s32[]{:T(128)S(6)} %select_n.13, f32[2,768,2048]{1,2,0:T(8,128)} %convolution_bitcast_fusion.2, pred[]{:T(512)S(6)} %compare.3), kind=kOutput, calls=%fused_computation.8.clone.1 | convolution fusion | flops 3225944064 | bytes 23068676 | tf_op jit(solution)/shard_map/while/body/eval_jaxpr/dot_general | solution.py:43
  260.3 11.5 %convolution_bitcast_fusion.2 = f32[2,768,2048]{1,2,0:T(8,128)} fusion(bf16[2,768,1024]{2,1,0:T(8,128)(2,1)S(1)} %get-tuple-element.156, bf16[12288,1024]{1,0:T(8,128)(2,1)} %get-tuple-element.155, s32[]{:T(128)S(6)} %select_n.13), kind=kOutput, calls=%fused_computation.2.clone.1 | convolution fusion | flops 6442450944 | bytes 19922948 | tf_op jit(solution)/shard_map/while/body/eval_jaxpr/qoa,ba->qob/dot_general | solution.py:39
  271.8 11.8 %select_add_fusion.2 = f32[768,1024]{1,0:T(8,128)} fusion(f32[768,1024]{1,0:T(8,128)} %get-tuple-element.146, bf16[12288,1024]{1,0:T(8,128)(2,1)} %get-tuple-element.155, s32[]{:T(128)S(6)} %select_n.13, f32[2,768,2048]{1,2,0:T(8,128)} %convolution_bitcast_fusion.2, pred[]{:T(512)S(6)} %compare.3), kind=kOutput, calls=%fused_computation.8.clone.1 | convolution fusion | flops 3225944064 | bytes 23068676 | tf_op jit(solution)/shard_map/while/body/eval_jaxpr/dot_general | solution.py:43
  283.6 11.5 %convolution_bitcast_fusion.2 = f32[2,768,2048]{1,2,0:T(8,128)} fusion(bf16[2,768,1024]{2,1,0:T(8,128)(2,1)S(1)} %get-tuple-element.156, bf16[12288,1024]{1,0:T(8,128)(2,1)} %get-tuple-element.155, s32[]{:T(128)S(6)} %select_n.13), kind=kOutput, calls=%fused_computation.2.clone.1 | convolution fusion | flops 6442450944 | bytes 19922948 | tf_op jit(solution)/shard_map/while/body/eval_jaxpr/qoa,ba->qob/dot_general | solution.py:39
  295.1 11.8 %select_add_fusion.2 = f32[768,1024]{1,0:T(8,128)} fusion(f32[768,1024]{1,0:T(8,128)} %get-tuple-element.146, bf16[12288,1024]{1,0:T(8,128)(2,1)} %get-tuple-element.155, s32[]{:T(128)S(6)} %select_n.13, f32[2,768,2048]{1,2,0:T(8,128)} %convolution_bitcast_fusion.2, pred[]{:T(512)S(6)} %compare.3), kind=kOutput, calls=%fused_computation.8.clone.1 | convolution fusion | flops 3225944064 | bytes 23068676 | tf_op jit(solution)/shard_map/while/body/eval_jaxpr/dot_general | solution.py:43
  306.9 11.5 %convolution_bitcast_fusion.2 = f32[2,768,2048]{1,2,0:T(8,128)} fusion(bf16[2,768,1024]{2,1,0:T(8,128)(2,1)S(1)} %get-tuple-element.156, bf16[12288,1024]{1,0:T(8,128)(2,1)} %get-tuple-element.155, s32[]{:T(128)S(6)} %select_n.13), kind=kOutput, calls=%fused_computation.2.clone.1 | convolution fusion | flops 6442450944 | bytes 19922948 | tf_op jit(solution)/shard_map/while/body/eval_jaxpr/qoa,ba->qob/dot_general | solution.py:39
  318.4 11.8 %select_add_fusion.2 = f32[768,1024]{1,0:T(8,128)} fusion(f32[768,1024]{1,0:T(8,128)} %get-tuple-element.146, bf16[12288,1024]{1,0:T(8,128)(2,1)} %get-tuple-element.155, s32[]{:T(128)S(6)} %select_n.13, f32[2,768,2048]{1,2,0:T(8,128)} %convolution_bitcast_fusion.2, pred[]{:T(512)S(6)} %compare.3), kind=kOutput, calls=%fused_computation.8.clone.1 | convolution fusion | flops 3225944064 | bytes 23068676 | tf_op jit(solution)/shard_map/while/body/eval_jaxpr/dot_general | solution.py:43
  330.2 6.1 %fusion.18 = f32[1024,1024]{1,0:T(8,128)} fusion(bf16[768,1024]{1,0:T(8,128)(2,1)} %param.8, f32[768,1024]{1,0:T(8,128)} %get-tuple-element.84), kind=kOutput, calls=%fused_computation.15 | convolution fusion | flops 1611399168 | bytes 8912896 | tf_op jit(solution)/shard_map/tsk,sl->ktl/dot_general | solution.py:61
  336.4 0.2 dynamic-slice_reduce_fusion
  336.6 72.7 %reduce-scatter.3.cloned.1.call-done = f32[64,1024]{1,0:T(8,128)} async-done(((f32[1024,1024]{1,0:T(8,128)}), f32[64,1024]{1,0:T(8,128)}) %reduce-scatter.3.cloned.1.call-update) | async-done | bytes 262160 | tf_op jit(solution)/shard_map/reduce_scatter | solution.py:60
  409.2 1.9 multiply_multiply_fusion
  411.1 13.9 %reduce-scatter.5.cloned.1.call-done = f32[1,64,1024]{2,1,0:T(8,128)} async-done(((f32[2,64,1024]{2,1,0:T(8,128)}), f32[1,64,1024]{2,1,0:T(8,128)}) %reduce-scatter.5.cloned.1.call-update) | async-done | bytes 262160 | tf_op jit(solution)/shard_map/reduce_scatter | solution.py:69
  (10 shorter events, 0.2 us)
Async XLA Ops:
  6.5 329.8 %copy-start = (f32[2,2]{1,0:T(2,128)S(1)}, f32[2,2]{1,0:T(2,128)}, u32[]{:S(2)}) copy-start(f32[2,2]{1,0:T(2,128)} %param.9) | copy-start | bytes 52
  6.5 56.1 %all-gather.5.cloned.1.call-start = ((), (), s32[]{:S(2)}) async-start(), calls=%async_computation.3 | async-start | bytes 4456448 | tf_op jit(solution)/shard_map/all_gather | solution.py:53
  8.3 183.1 %all-gather.3.cloned.1.call-start = ((), (), s32[]{:S(2)}) async-start(), calls=%async_computation.2 | async-start | bytes 26738688 | tf_op jit(solution)/shard_map/all_gather | solution.py:58
  9.0 400.2 %reduce-scatter.3.cloned.1.call-start = ((), (), s32[]{:S(2)}) async-start(), calls=%async_computation.4 | async-start | bytes 4456448 | tf_op jit(solution)/shard_map/reduce_scatter | solution.py:60
  336.3 88.8 %reduce-scatter.5.cloned.1.call-start = ((), (), s32[]{:S(2)}) async-start(), calls=%async_computation.5 | async-start | bytes 786432 | tf_op jit(solution)/shard_map/reduce_scatter | solution.py:69
Sparse Core Ops, SparseCore 0:
  9.5 53.1 all-gather.4
  64.3 127.0 all-gather.2
  336.4 72.7 reduce-scatter.2
  411.3 13.6 reduce-scatter.4
where the time goes:
time: 432 us
  waiting for transfers between devices  259 us (60%)
  matrix products  153 us (35%)
  between operations  13.2 us (3%)
    all_gather x1, waiting for transfers between devices, shards(): lax.all_gather(basis, 'grid', axis=0, tiled=True)  118 us
    reduce_scatter x1, waiting for transfers between devices, shards(): lax.psum_scatter(jnp.einsum('tsk,sl->ktl', back_half, basis, preferred_el...  72.7 us
    dot_general x6, matrix products, one_step(): jnp.dot(product, basis_subpart, preferred_element_type=jnp.float32)  69.8 us
    dot_general x6, matrix products, one_step(): jnp.einsum('qoa,ba->qob', combined_rows, basis_subpart, preferred_element...  69 us
    all_gather x1, waiting for transfers between devices, shards(): lax.all_gather(stacked, 'grid', axis=2, tiled=True)  53.6 us
    reduce_scatter x1, waiting for transfers between devices, shards(): lax.psum_scatter(weigh_times(time_weights, block_list, scale_factor), 'tm...  13.9 us
  transfers between devices with their start and end apart: 4, of which 4 were waited for; matrix products, arithmetic and copies ran while one was open for 3% of the time, Pallas kernels for 0%

commit v1 on v0

--- a/solution.py
+++ b/solution.py
@@ -47,11 +47,24 @@
         return accumulate
 
     initial = jnp.zeros((time_count * row_total, NB), jnp.float32)
+
+    def render_task(array_in, in_dim):
+        current_block = lax.axis_size("grid")
+        upper = lax.axis_index("grid")
+        r2, earlier = (current_block, upper)
+        z2, local_next = (array_in, 1)
+        while local_next < r2:
+            e_next = lax.ppermute(
+                z2, axis_name="grid", perm=[(d, d ^ local_next) for d in range(r2)]
+            )
+            b_now = jnp.concatenate([z2, e_next], axis=in_dim)
+            state_now = jnp.concatenate([e_next, z2], axis=in_dim)
+            z2 = jnp.where(earlier & local_next == 0, b_now, state_now)
+            local_next = 2 * local_next
+        return z2
+
     projected = jnp.einsum(
-        "sl,ftkl->ftsk",
-        basis,
-        lax.all_gather(stacked, "grid", axis=2, tiled=True),
-        preferred_element_type=jnp.float32,
+        "sl,ftkl->ftsk", basis, render_task(stacked, 2), preferred_element_type=jnp.float32
     ).astype(jnp.bfloat16)
     combined_rows = projected.reshape(2, time_count * row_total, NB)
     accumulate = make_accumulate(combined_rows)

time: 432 us -> 439 us (1.016)
  matrix products: 153 us -> 100 us
  waiting for transfers between devices: 259 us -> 296 us
  local copies, waits for them, and re-layouts: 3.4 us -> 13.7 us
  other arithmetic: 3.57 us -> 9.73 us
  starting transfers between devices: 0.12 us -> 5.87 us
    ppermute x0 -> x4, waiting for transfers between devices: none -> 201 us  [render_task(): lax.ppermute(z2, axis_name='grid', perm=[(d, d ^ local_next) for d in ran...]
    all_gather x1, waiting for transfers between devices: 118 us -> 0.02 us  [shards(): lax.all_gather(basis, 'grid', axis=0, tiled=True)]
    all_gather x1 -> x0, waiting for transfers between devices: 53.6 us -> none  [shards(): lax.all_gather(stacked, 'grid', axis=2, tiled=True)]
    dot_general x6, matrix products: 69.8 us -> 33.9 us  [one_step(): jnp.dot(product, basis_subpart, preferred_element_type=jnp.float32)]
    dot_general x6, matrix products: 69 us -> 52.4 us  [one_step(): jnp.einsum('qoa,ba->qob', combined_rows, basis_subpart, preferred_element...]
    while x0 -> x24, local copies, waits for them, and re-layouts: none -> 10.3 us
    reduce_scatter x1, waiting for transfers between devices: 72.7 us -> 79.8 us  [shards(): lax.psum_scatter(jnp.einsum('tsk,sl->ktl', back_half, basis, preferred_el...]
    select_n x0 -> x6, other arithmetic: none -> 6.86 us  [render_task(): z2 = jnp.where(earlier & local_next == 0, b_now, state_now)]
  transfers between devices with their start and end apart: 4 -> 7, of which waited for: 4 -> 6; matrix products, arithmetic and copies ran while one was open for 3% -> 4% of each run, Pallas kernels for 0% -> 0%
where the time goes in v1:
time: 439 us
  waiting for transfers between devices  296 us (67%)
  matrix products  100 us (23%)
  local copies, waits for them, and re-layouts  13.7 us (3%)
  between operations  13.2 us (3%)
  other arithmetic  9.73 us (2%)
  starting transfers between devices  5.87 us (1%)
    ppermute x4, waiting for transfers between devices, render_task(): lax.ppermute(z2, axis_name='grid', perm=[(d, d ^ local_next) for d in ran...  201 us
    reduce_scatter x1, waiting for transfers between devices, shards(): lax.psum_scatter(jnp.einsum('tsk,sl->ktl', back_half, basis, preferred_el...  79.8 us
    dot_general x6, matrix products, one_step(): jnp.einsum('qoa,ba->qob', combined_rows, basis_subpart, preferred_element...  52.4 us
    dot_general x6, matrix products, one_step(): jnp.dot(product, basis_subpart, preferred_element_type=jnp.float32)  33.9 us
    reduce_scatter x1, waiting for transfers between devices, shards(): lax.psum_scatter(weigh_times(time_weights, block_list, scale_factor), 'tm...  14 us
    while x24, local copies, waits for them, and re-layouts  10.3 us
  transfers between devices with their start and end apart: 7, of which 6 were waited for; matrix products, arithmetic and copies ran while one was open for 4% of the time, Pallas kernels for 0%

profile of v1, /device:TPU:0, one launch (start us, length us, event | category | flops | bytes accessed | tf_op | source)
XLA Modules:
  0.0 438.8 jit_solution(10422748852394842231)
XLA Ops:
  11.2 2.9 collective-permute-start.1
  14.3 19.8 %collective-permute-done.1 = bf16[2,1,128,1024]{3,2,1,0:T(8,128)(2,1)S(1)} collective-permute-done((bf16[2,1,128,1024]{3,2,1,0:T(8,128)(2,1)S(1)}, bf16[2,1,128,1024]{3,2,1,0:T(8,128)(2,1)S(1)}, u32[]{:S(2)}, u32[]{:S(2)}) %collective-permute-start.1) | collective-permute-done | bytes 524320 | tf_op jit(solution)/shard_map/ppermute | solution.py:57
  36.1 47.1 %collective-permute-done.2 = bf16[2,1,256,1024]{3,2,1,0:T(8,128)(2,1)S(1)} collective-permute-done((bf16[2,1,256,1024]{3,2,1,0:T(8,128)(2,1)}, bf16[2,1,256,1024]{3,2,1,0:T(8,128)(2,1)S(1)}, u32[]{:S(2)}, u32[]{:S(2)}) %collective-permute-start.2) | collective-permute-done | bytes 1048608 | tf_op jit(solution)/shard_map/ppermute | solution.py:57
  83.2 2.5 fusion.20
  85.8 2.3 collective-permute-start.3
  89.1 133.3 %collective-permute-done.3 = bf16[2,1,512,1024]{3,2,1,0:T(8,128)(2,1)} collective-permute-done((bf16[2,1,512,1024]{3,2,1,0:T(8,128)(2,1)}, bf16[2,1,512,1024]{3,2,1,0:T(8,128)(2,1)}, u32[]{:S(2)}, u32[]{:S(2)}) %collective-permute-start.3) | collective-permute-done | bytes 2097184 | tf_op jit(solution)/shard_map/ppermute | solution.py:57
  222.3 7.8 %convert_bitcast_fusion = bf16[2,768,1024]{1,2,0:T(8,128)(2,1)} fusion(bf16[2,512,1024]{2,1,0:T(8,128)(2,1)} %bitcast.18, bf16[2,512,1024]{2,1,0:T(8,128)(2,1)S(1)} %maximum_select_fusion.4, pred[]{:T(512)S(6)} %eq.12, bf16[768,1024]{1,0:T(8,128)(2,1)S(1)} %copy-done.1), kind=kOutput, calls=%fused_computation.19 | convolution fusion | flops 3241672704 | bytes 8912897 | tf_op jit(solution)/shard_map/sl,ftkl->ftsk/dot_general | solution.py:66
  230.1 3.2 copy.15
  233.3 96.8 %while.14 = (s32[]{:T(128)}, f32[768,1024]{1,0:T(8,128)}, bf16[12288,1024]{1,0:T(8,128)(2,1)}, bf16[2,768,1024]{2,1,0:T(8,128)(2,1)S(1)}, s32[]{:T(128)}, /*index=5*/s32[]{:T(128)}, s32[]{:T(128)}, s32[]{:T(128)}) while((s32[]{:T(128)}, f32[768,1024]{1,0:T(8,128)}, bf16[12288,1024]{1,0:T(8,128)(2,1)}, ...), condition=%wide.region_1.2_spmd.clone, body=%wide.region_0.1_spmd.clone.sunk | while | flops 9668395008 | bytes 68157656 | solution.py:45
  233.4 8.7 %convolution_bitcast_fusion.2 = f32[2,768,2048]{1,2,0:T(8,128)S(1)} fusion(bf16[2,768,1024]{2,1,0:T(8,128)(2,1)S(1)} %get-tuple-element.158, bf16[12288,1024]{1,0:T(8,128)(2,1)} %get-tuple-element.157, s32[]{:T(128)S(6)} %select_n.144), kind=kOutput, calls=%fused_computation.2.clone.1 | convolution fusion | flops 6442450944 | bytes 19922948 | tf_op jit(solution)/shard_map/while/body/eval_jaxpr/qoa,ba->qob/dot_general | solution.py:39
  242.1 5.7 %select_add_fusion.2 = f32[768,1024]{1,0:T(8,128)S(1)} fusion(f32[768,1024]{1,0:T(8,128)S(1)} %copy-done.2, bf16[12288,1024]{1,0:T(8,128)(2,1)} %get-tuple-element.157, s32[]{:T(128)S(6)} %select_n.144, f32[2,768,2048]{1,2,0:T(8,128)S(1)} %convolution_bitcast_fusion.2, pred[]{:T(512)S(6)} %compare.3), kind=kOutput, calls=%fused_computation.8.clone.1 | convolution fusion | flops 3225944064 | bytes 23068676 | tf_op jit(solution)/shard_map/while/body/eval_jaxpr/dot_general | solution.py:43
  249.5 8.7 %convolution_bitcast_fusion.2 = f32[2,768,2048]{1,2,0:T(8,128)S(1)} fusion(bf16[2,768,1024]{2,1,0:T(8,128)(2,1)S(1)} %get-tuple-element.158, bf16[12288,1024]{1,0:T(8,128)(2,1)} %get-tuple-element.157, s32[]{:T(128)S(6)} %select_n.144), kind=kOutput, calls=%fused_computation.2.clone.1 | convolution fusion | flops 6442450944 | bytes 19922948 | tf_op jit(solution)/shard_map/while/body/eval_jaxpr/qoa,ba->qob/dot_general | solution.py:39
  258.3 5.7 %select_add_fusion.2 = f32[768,1024]{1,0:T(8,128)S(1)} fusion(f32[768,1024]{1,0:T(8,128)S(1)} %copy-done.2, bf16[12288,1024]{1,0:T(8,128)(2,1)} %get-tuple-element.157, s32[]{:T(128)S(6)} %select_n.144, f32[2,768,2048]{1,2,0:T(8,128)S(1)} %convolution_bitcast_fusion.2, pred[]{:T(512)S(6)} %compare.3), kind=kOutput, calls=%fused_computation.8.clone.1 | convolution fusion | flops 3225944064 | bytes 23068676 | tf_op jit(solution)/shard_map/while/body/eval_jaxpr/dot_general | solution.py:43
  265.6 8.7 %convolution_bitcast_fusion.2 = f32[2,768,2048]{1,2,0:T(8,128)S(1)} fusion(bf16[2,768,1024]{2,1,0:T(8,128)(2,1)S(1)} %get-tuple-element.158, bf16[12288,1024]{1,0:T(8,128)(2,1)} %get-tuple-element.157, s32[]{:T(128)S(6)} %select_n.144), kind=kOutput, calls=%fused_computation.2.clone.1 | convolution fusion | flops 6442450944 | bytes 19922948 | tf_op jit(solution)/shard_map/while/body/eval_jaxpr/qoa,ba->qob/dot_general | solution.py:39
  274.4 5.7 %select_add_fusion.2 = f32[768,1024]{1,0:T(8,128)S(1)} fusion(f32[768,1024]{1,0:T(8,128)S(1)} %copy-done.2, bf16[12288,1024]{1,0:T(8,128)(2,1)} %get-tuple-element.157, s32[]{:T(128)S(6)} %select_n.144, f32[2,768,2048]{1,2,0:T(8,128)S(1)} %convolution_bitcast_fusion.2, pred[]{:T(512)S(6)} %compare.3), kind=kOutput, calls=%fused_computation.8.clone.1 | convolution fusion | flops 3225944064 | bytes 23068676 | tf_op jit(solution)/shard_map/while/body/eval_jaxpr/dot_general | solution.py:43
  281.8 8.7 %convolution_bitcast_fusion.2 = f32[2,768,2048]{1,2,0:T(8,128)S(1)} fusion(bf16[2,768,1024]{2,1,0:T(8,128)(2,1)S(1)} %get-tuple-element.158, bf16[12288,1024]{1,0:T(8,128)(2,1)} %get-tuple-element.157, s32[]{:T(128)S(6)} %select_n.144), kind=kOutput, calls=%fused_computation.2.clone.1 | convolution fusion | flops 6442450944 | bytes 19922948 | tf_op jit(solution)/shard_map/while/body/eval_jaxpr/qoa,ba->qob/dot_general | solution.py:39
  290.5 5.7 %select_add_fusion.2 = f32[768,1024]{1,0:T(8,128)S(1)} fusion(f32[768,1024]{1,0:T(8,128)S(1)} %copy-done.2, bf16[12288,1024]{1,0:T(8,128)(2,1)} %get-tuple-element.157, s32[]{:T(128)S(6)} %select_n.144, f32[2,768,2048]{1,2,0:T(8,128)S(1)} %convolution_bitcast_fusion.2, pred[]{:T(512)S(6)} %compare.3), kind=kOutput, calls=%fused_computation.8.clone.1 | convolution fusion | flops 3225944064 | bytes 23068676 | tf_op jit(solution)/shard_map/while/body/eval_jaxpr/dot_general | solution.py:43
  297.9 8.7 %convolution_bitcast_fusion.2 = f32[2,768,2048]{1,2,0:T(8,128)S(1)} fusion(bf16[2,768,1024]{2,1,0:T(8,128)(2,1)S(1)} %get-tuple-element.158, bf16[12288,1024]{1,0:T(8,128)(2,1)} %get-tuple-element.157, s32[]{:T(128)S(6)} %select_n.144), kind=kOutput, calls=%fused_computation.2.clone.1 | convolution fusion | flops 6442450944 | bytes 19922948 | tf_op jit(solution)/shard_map/while/body/eval_jaxpr/qoa,ba->qob/dot_general | solution.py:39
  306.6 5.7 %select_add_fusion.2 = f32[768,1024]{1,0:T(8,128)S(1)} fusion(f32[768,1024]{1,0:T(8,128)S(1)} %copy-done.2, bf16[12288,1024]{1,0:T(8,128)(2,1)} %get-tuple-element.157, s32[]{:T(128)S(6)} %select_n.144, f32[2,768,2048]{1,2,0:T(8,128)S(1)} %convolution_bitcast_fusion.2, pred[]{:T(512)S(6)} %compare.3), kind=kOutput, calls=%fused_computation.8.clone.1 | convolution fusion | flops 3225944064 | bytes 23068676 | tf_op jit(solution)/shard_map/while/body/eval_jaxpr/dot_general | solution.py:43
  314.0 8.7 %convolution_bitcast_fusion.2 = f32[2,768,2048]{1,2,0:T(8,128)S(1)} fusion(bf16[2,768,1024]{2,1,0:T(8,128)(2,1)S(1)} %get-tuple-element.158, bf16[12288,1024]{1,0:T(8,128)(2,1)} %get-tuple-element.157, s32[]{:T(128)S(6)} %select_n.144), kind=kOutput, calls=%fused_computation.2.clone.1 | convolution fusion | flops 6442450944 | bytes 19922948 | tf_op jit(solution)/shard_map/while/body/eval_jaxpr/qoa,ba->qob/dot_general | solution.py:39
  322.8 5.7 %select_add_fusion.2 = f32[768,1024]{1,0:T(8,128)S(1)} fusion(f32[768,1024]{1,0:T(8,128)S(1)} %copy-done.2, bf16[12288,1024]{1,0:T(8,128)(2,1)} %get-tuple-element.157, s32[]{:T(128)S(6)} %select_n.144, f32[2,768,2048]{1,2,0:T(8,128)S(1)} %convolution_bitcast_fusion.2, pred[]{:T(512)S(6)} %compare.3), kind=kOutput, calls=%fused_computation.8.clone.1 | convolution fusion | flops 3225944064 | bytes 23068676 | tf_op jit(solution)/shard_map/while/body/eval_jaxpr/dot_general | solution.py:43
  330.1 6.1 %fusion.22 = f32[1024,1024]{1,0:T(8,128)} fusion(bf16[768,1024]{1,0:T(8,128)(2,1)} %param.8, f32[768,1024]{1,0:T(8,128)} %get-tuple-element.84), kind=kOutput, calls=%fused_computation.24 | convolution fusion | flops 1611399168 | bytes 8912896 | tf_op jit(solution)/shard_map/tsk,sl->ktl/dot_general | solution.py:74
  336.6 79.8 %reduce-scatter.3.cloned.1.call-done = f32[64,1024]{1,0:T(8,128)} async-done(((f32[1024,1024]{1,0:T(8,128)}), f32[64,1024]{1,0:T(8,128)}) %reduce-scatter.3.cloned.1.call-update) | async-done | bytes 262160 | tf_op jit(solution)/shard_map/reduce_scatter | solution.py:73
  418.3 14.0 %reduce-scatter.5.cloned.1.call-done = f32[1,64,1024]{2,1,0:T(8,128)} async-done(((f32[2,64,1024]{2,1,0:T(8,128)}), f32[1,64,1024]{2,1,0:T(8,128)}) %reduce-scatter.5.cloned.1.call-update) | async-done | bytes 262160 | tf_op jit(solution)/shard_map/reduce_scatter | solution.py:82
  (47 shorter events, 20.2 us)
Async XLA Ops:
  6.5 329.8 %copy-start = (f32[2,2]{1,0:T(2,128)S(1)}, f32[2,2]{1,0:T(2,128)}, u32[]{:S(2)}) copy-start(f32[2,2]{1,0:T(2,128)} %param.9) | copy-start | bytes 52
  6.5 226.8 %all-gather.2.cloned.1.call-start = ((), (), s32[]{:S(2)}) async-start(), calls=%async_computation.2 | async-start | bytes 26738688 | tf_op jit(solution)/shard_map/all_gather | solution.py:71
  7.3 409.1 %reduce-scatter.3.cloned.1.call-start = ((), (), s32[]{:S(2)}) async-start(), calls=%async_computation.3 | async-start | bytes 4456448 | tf_op jit(solution)/shard_map/reduce_scatter | solution.py:73
  8.3 1.7 collective-permute-start
  11.2 22.8 %collective-permute-start.1 = (bf16[2,1,128,1024]{3,2,1,0:T(8,128)(2,1)S(1)}, bf16[2,1,128,1024]{3,2,1,0:T(8,128)(2,1)S(1)}, u32[]{:S(2)}, u32[]{:S(2)}) collective-permute-start(bf16[2,1,128,1024]{3,2,1,0:T(8,128)(2,1)S(1)} %fusion.25), channel_id=1, source_target_pairs={{0,2},{1,3},{2,0},{3,1},{4,6},{5,7},{6,4},{7,5},{8,10},{9,11},{10,... | collective-permute-start | bytes 1572872 | tf_op jit(solution)/shard_map/ppermute | solution.py:57
  35.6 47.6 %collective-permute-start.2 = (bf16[2,1,256,1024]{3,2,1,0:T(8,128)(2,1)}, bf16[2,1,256,1024]{3,2,1,0:T(8,128)(2,1)S(1)}, u32[]{:S(2)}, u32[]{:S(2)}) collective-permute-start(bf16[2,1,256,1024]{3,2,1,0:T(8,128)(2,1)} %fusion.24), channel_id=1, source_target_pairs={{0,4},{1,5},{2,6},{3,7},{4,0},{5,1},{6,2},{7,3},{8,12},{9,13},{10,... | collective-permute-start | bytes 3145736 | tf_op jit(solution)/shard_map/ppermute | solution.py:57
  85.8 136.6 %collective-permute-start.3 = (bf16[2,1,512,1024]{3,2,1,0:T(8,128)(2,1)}, bf16[2,1,512,1024]{3,2,1,0:T(8,128)(2,1)}, u32[]{:S(2)}, u32[]{:S(2)}) collective-permute-start(bf16[2,1,512,1024]{3,2,1,0:T(8,128)(2,1)} %fusion.20), channel_id=1, source_target_pairs={{0,8},{1,9},{2,10},{3,11},{4,12},{5,13},{6,14},{7,15},{8,0},{9,1},... | collective-permute-start | bytes 6291464 | tf_op jit(solution)/shard_map/ppermute | solution.py:57
  88.0 134.3 %copy-start.1 = (bf16[768,1024]{1,0:T(8,128)(2,1)S(1)}, bf16[768,1024]{1,0:T(8,128)(2,1)}, u32[]{:S(2)}) copy-start(bf16[768,1024]{1,0:T(8,128)(2,1)} %param.8) | copy-start | bytes 4718596
  233.4 8.7 %copy-start.2 = (f32[768,1024]{1,0:T(8,128)S(1)}, f32[768,1024]{1,0:T(8,128)}, u32[]{:S(2)}) copy-start(f32[768,1024]{1,0:T(8,128)} %get-tuple-element.148) | copy-start | bytes 9437188 | tf_op jit(solution)/shard_map/while
  247.8 1.7 copy-start.3
  249.5 8.7 %copy-start.2 = (f32[768,1024]{1,0:T(8,128)S(1)}, f32[768,1024]{1,0:T(8,128)}, u32[]{:S(2)}) copy-start(f32[768,1024]{1,0:T(8,128)} %get-tuple-element.148) | copy-start | bytes 9437188 | tf_op jit(solution)/shard_map/while
  263.9 1.7 copy-start.3
  265.6 8.7 %copy-start.2 = (f32[768,1024]{1,0:T(8,128)S(1)}, f32[768,1024]{1,0:T(8,128)}, u32[]{:S(2)}) copy-start(f32[768,1024]{1,0:T(8,128)} %get-tuple-element.148) | copy-start | bytes 9437188 | tf_op jit(solution)/shard_map/while
  280.0 1.7 copy-start.3
  281.8 8.7 %copy-start.2 = (f32[768,1024]{1,0:T(8,128)S(1)}, f32[768,1024]{1,0:T(8,128)}, u32[]{:S(2)}) copy-start(f32[768,1024]{1,0:T(8,128)} %get-tuple-element.148) | copy-start | bytes 9437188 | tf_op jit(solution)/shard_map/while
  296.2 1.7 copy-start.3
  297.9 8.7 %copy-start.2 = (f32[768,1024]{1,0:T(8,128)S(1)}, f32[768,1024]{1,0:T(8,128)}, u32[]{:S(2)}) copy-start(f32[768,1024]{1,0:T(8,128)} %get-tuple-element.148) | copy-start | bytes 9437188 | tf_op jit(solution)/shard_map/while
  312.3 1.7 copy-start.3
  314.0 8.7 %copy-start.2 = (f32[768,1024]{1,0:T(8,128)S(1)}, f32[768,1024]{1,0:T(8,128)}, u32[]{:S(2)}) copy-start(f32[768,1024]{1,0:T(8,128)} %get-tuple-element.148) | copy-start | bytes 9437188 | tf_op jit(solution)/shard_map/while
  328.4 1.7 copy-start.3
  336.3 96.0 %reduce-scatter.5.cloned.1.call-start = ((), (), s32[]{:S(2)}) async-start(), calls=%async_computation.4 | async-start | bytes 786432 | tf_op jit(solution)/shard_map/reduce_scatter | solution.py:82
Sparse Core Ops, SparseCore 0:
  8.9 221.4 all-gather.1
  336.4 79.8 reduce-scatter.2
  418.6 13.6 reduce-scatter.4
